TPU v7x, 256 devices: a whole 4x4x8 slice. The times are simulated.
256 devices in a mesh: shard: 16 (over x, z_hi, core), rep: 16 (over y, z_lo).
Axes of the slice: x: 4, y: 4, z: 8 (z_hi: 2, z_lo: 4; z = z_hi * 4 + z_lo), core: 2. Of those that a mesh axis runs over, the one named last changes fastest.
Arguments:
- grads: bfloat16 [16, 16, 2097152], P('shard', 'rep'), may hold values from -5000 to 5000
- momentum_codes: int32 [2097152], P(('shard', 'rep')), may hold values from -127 to 127
- variance_codes: int32 [2097152], P(('shard', 'rep')), may hold values from 16 to 255
- momentum_scale: float32 [1280], P(('shard', 'rep')), may hold values from 0.5 to 4, as said below
- variance_scale: float32 [1280], P(('shard', 'rep')), may hold values from 1 to 4, as said below
- master: float32 [2097152], P(('shard', 'rep')), may hold values from -2.5 to 2.5
- step: int32 [1], replicated, may hold values from 1 to 19
Outputs:
- new_master: float32 [2097152], P(('shard', 'rep'))
- weights: bfloat16 [2097152], P('shard')
- update: float32 [2097152], P(('shard', 'rep'))
- momentum_norm: float32 [2097152], P(('shard', 'rep'))
- variance_norm: float32 [2097152], P(('shard', 'rep'))
- momentum_absmax: float32 [1280], P(('shard', 'rep'))
- variance_absmax: float32 [1280], P(('shard', 'rep'))
Inputs may be any that keep to these rules, and one draw needn't show every extreme that they name: `momentum_scale`: A block touched by two neighbouring devices has the same value in both devices' slots. `variance_scale`: A block touched by two neighbouring devices has the same value in both devices' slots.
All inputs are finite; a program needn't handle non-finite values.
Results may differ from a plain program's by a relative error of at most 0.0004.
Values may be sent and summed in bfloat16 or wider, within the bound.
A program may use at most 64 MiB of HBM per device.

v0:
```python
import jax
import jax.numpy as jnp
from jax import lax
from jax.sharding import PartitionSpec as P

BLOCK = 2048


def extended(block, sides, width):
    for axis, dim in sides:
        count = lax.axis_size(axis)
        forward = [(i, i + 1) for i in range(count - 1)]
        backward = [(target, source) for source, target in forward]
        low = lax.ppermute(
            lax.slice_in_dim(block, block.shape[dim] - width, None, axis=dim), axis, forward
        )
        high = lax.ppermute(lax.slice_in_dim(block, 0, width, axis=dim), axis, backward)
        block = jnp.concatenate([low, block, high], axis=dim)
    return block


def on_device(grads, momentum_codes, variance_codes, momentum_scale, variance_scale, master, step):
    own_len = master.shape[0]
    slot_count = momentum_scale.shape[0]
    block_len = BLOCK
    half_len = block_len // 2
    shard_count = lax.axis_size("shard")
    rep_count = lax.axis_size("rep")
    grad_terms = grads.reshape(-1).astype(jnp.float32)
    partial_sum = lax.psum_scatter(grad_terms, "shard", scatter_dimension=0, tiled=True)
    gsum = lax.psum_scatter(partial_sum, "rep", scatter_dimension=0, tiled=True)
    norm_sq = lax.psum(jnp.sum(gsum * gsum), ("shard", "rep"))
    total_params = own_len * shard_count * rep_count
    clip_factor = jnp.minimum(1.0, float(total_params) ** 0.5 / (jnp.sqrt(norm_sq) + 1e-06))
    scaled = gsum * clip_factor

    def spread(scale_table):
        return jnp.repeat(scale_table, block_len)[half_len : half_len + own_len]

    m_old = momentum_codes.astype(jnp.float32) / 127.0 * spread(momentum_scale)
    v_old = variance_codes.astype(jnp.float32) / 255.0 * spread(variance_scale)
    momentum = 0.9 * m_old + 0.1 * scaled
    variance = 0.95 * v_old + 0.05 * scaled * scaled
    count = step[0].astype(jnp.float32)
    first_fix = 1.0 - jnp.power(jnp.float32(0.9), count)
    second_fix = 1.0 - jnp.power(jnp.float32(0.95), count)
    update = momentum / first_fix / (jnp.sqrt(variance / second_fix) + 1e-08)
    new_master = master * (1.0 - 0.0001 * 0.1) - 0.0001 * update
    weights = lax.all_gather(new_master.astype(jnp.bfloat16), "rep", axis=0, tiled=True)

    def slot_max(values):
        padded = jnp.pad(jnp.abs(values), (half_len, half_len))
        return jnp.max(padded.reshape(slot_count, block_len), axis=1)

    m_table = slot_max(momentum)
    v_table = slot_max(variance)
    own_edge = jnp.stack(
        [jnp.stack([m_table[0], v_table[0]]), jnp.stack([m_table[-1], v_table[-1]])]
    )
    rim_vals = extended(own_edge, ((("shard", "rep"), 0),), 1)
    m_table = m_table.at[0].max(rim_vals[0, 0]).at[-1].max(rim_vals[3, 0])
    v_table = v_table.at[0].max(rim_vals[0, 1]).at[-1].max(rim_vals[3, 1])
    momentum_norm = momentum / (spread(m_table) + 1e-06)
    variance_norm = variance / (spread(v_table) + 1e-06)
    return (new_master, weights, update, momentum_norm, variance_norm, m_table, v_table)


def solution(mesh):
    in_specs = (
        P("shard", "rep", None),
        P(("shard", "rep")),
        P(("shard", "rep")),
        P(("shard", "rep")),
        P(("shard", "rep")),
        P(("shard", "rep")),
        P(),
    )
    out_specs = (
        P(("shard", "rep")),
        P("shard"),
        P(("shard", "rep")),
        P(("shard", "rep")),
        P(("shard", "rep")),
        P(("shard", "rep")),
        P(("shard", "rep")),
    )
    return jax.shard_map(
        on_device, mesh=mesh, in_specs=in_specs, out_specs=out_specs, check_vma=False
    )
```

profile of v0, /device:TPU:2, one launch (start us, length us, event | category | flops | bytes accessed | tf_op | source)
XLA Modules:
  0.0 717.0 jit_solution(4956482309576053359)
XLA Ops:
  7.2 10.8 %convert_element_type.28 = f32[1,1,2097152]{2,1,0:T(1,128)} convert(bf16[1,1,2097152]{2,1,0:T(2,128)(2,1)} %param.15) | non-fusion elementwise | flops 2097152 | bytes 12582912 | tf_op jit(solution)/shard_map/convert_element_type | solution.py:29
  20.0 379.7 %all-reduce.7.cloned.1.call-done = f32[2097152]{0:T(1024)} async-done(((f32[2097152]{0:T(1024)}), f32[2097152]{0:T(1024)}) %all-reduce.7.cloned.1.call-update) | async-done | bytes 8388624
  399.7 1.9 dynamic-slice.25
  401.7 0.6 dynamic-slice.26
  403.8 161.5 %all-reduce.9.cloned.1.call-done = f32[131072]{0:T(1024)} async-done(((f32[131072]{0:T(1024)}), f32[131072]{0:T(1024)}) %all-reduce.9.cloned.1.call-update) | async-done | bytes 524304
  565.3 1.4 multiply_reduce_fusion
  566.7 75.3 %psum.7 = f32[]{:T(128)} all-reduce(f32[]{:T(128)} %multiply_reduce_fusion), channel_id=1, replica_groups=mesh['shard'=16,'rep'=16] {'shard','rep'}, use_global_device_ids=true, to_apply=%region_3.0 | all-reduce | flops 1 | bytes 8 | tf_op jit(solution)/shard_map/psum | solution.py:32
  642.7 0.8 fusion.6
  643.7 0.6 slice.84
  644.4 0.6 slice.83
  645.0 1.4 maximum_bitcast_fusion
  646.4 1.9 collective-permute-start
  648.3 7.2 %collective-permute-done = f32[1,2]{1,0:T(1,128)S(1)} collective-permute-done((f32[1,2]{1,0:T(1,128)S(1)}, f32[1,2]{1,0:T(1,128)S(1)}, u32[]{:S(2)}, u32[]{:S(2)}) %collective-permute-start) | collective-permute-done | bytes 40 | tf_op jit(solution)/shard_map/ppermute | solution.py:14
  655.5 0.6 fusion.12
  656.0 1.8 constant_dynamic-update-slice_fusion.2
  657.9 1.4 maximum_bitcast_fusion.1
  659.2 1.9 collective-permute-start.1
  661.1 3.5 collective-permute-done.1
  664.7 0.6 fusion.11
  665.3 0.8 constant_dynamic-update-slice_fusion
  666.1 0.8 constant_dynamic-update-slice_fusion.1
  667.1 0.7 fusion.10
  667.7 41.7 %all_gather.3 = bf16[131072]{0:T(1024)(128)(2,1)S(1)} all-gather(bf16[8192]{0:T(1024)(128)(2,1)S(1)} %get-tuple-element.59), channel_id=1, replica_groups=mesh['shard'=16,'rep'=16] {'rep'}, dimensions={0}, use_global_device_ids=true | all-gather | bytes 278528 | tf_op jit(solution)/shard_map/all_gather | solution.py:49
  709.5 0.7 copy.22
  (37 shorter events, 1.9 us)
Async XLA Ops:
  7.2 392.5 %all-reduce.7.cloned.1.call-start = ((), (), s32[]{:S(2)}) async-start(), calls=%async_computation | async-start | bytes 16777216
  18.1 0.7 copy-start.8
  18.1 383.6 %copy-start.7 = (u32[256]{0:T(256)S(1)}, u32[256]{0:T(256)}, u32[]{:S(2)}) copy-start(u32[256]{0:T(256)} %constant.134) | copy-start | bytes 3076
  18.1 384.2 %copy-start.5 = (f32[5]{0:T(128)S(1)}, f32[5]{0:T(128)}, u32[]{:S(2)}) copy-start(f32[5]{0:T(128)} %param.19) | copy-start | bytes 64
  18.1 384.3 %copy-start.6 = (f32[5]{0:T(128)S(1)}, f32[5]{0:T(128)}, u32[]{:S(2)}) copy-start(f32[5]{0:T(128)} %param.18) | copy-start | bytes 64
  18.1 624.6 %copy-start = (s32[8192]{0:T(1024)S(1)}, s32[8192]{0:T(1024)}, u32[]{:S(2)}) copy-start(s32[8192]{0:T(1024)} %param.17) | copy-start | bytes 98308
  18.1 624.6 %copy-start.1 = (s32[8192]{0:T(1024)S(1)}, s32[8192]{0:T(1024)}, u32[]{:S(2)}) copy-start(s32[8192]{0:T(1024)} %param.16) | copy-start | bytes 98308
  18.1 648.9 %copy-start.2 = (f32[8192]{0:T(1024)S(1)}, f32[8192]{0:T(1024)}, u32[]{:S(2)}) copy-start(f32[8192]{0:T(1024)} %param.20) | copy-start | bytes 98308
  18.2 547.1 %all-reduce.9.cloned.1.call-start = ((), (), s32[]{:S(2)}) async-start(), calls=%async_computation.1 | async-start | bytes 1048576
  646.4 9.1 %collective-permute-start = (f32[1,2]{1,0:T(1,128)S(1)}, f32[1,2]{1,0:T(1,128)S(1)}, u32[]{:S(2)}, u32[]{:S(2)}) collective-permute-start(f32[1,2]{1,0:T(1,128)S(1)} %maximum_bitcast_fusion), channel_id=1, source_target_pairs={{0,1},{1,2},{2,3},{3,4},{4,5},{5,6},{6,7},{7,8},{8,9},{9,10},{10,1... | collective-permute-start | bytes 32 | tf_op jit(solution)/shard_map/ppermute | solution.py:14
  659.2 5.5 collective-permute-start.1
  666.1 44.2 %copy-start.3 = (f32[5]{0:T(128)}, f32[5]{0:T(128)S(1)}, u32[]{:S(2)}) copy-start(f32[5]{0:T(128)S(1)} %constant_dynamic-update-slice_fusion) | copy-start | bytes 64
  666.9 43.3 %copy-start.4 = (f32[5]{0:T(128)}, f32[5]{0:T(128)S(1)}, u32[]{:S(2)}) copy-start(f32[5]{0:T(128)S(1)} %constant_dynamic-update-slice_fusion.1) | copy-start | bytes 64
Sparse Core Ops, SparseCore 0:
  18.3 381.3 all-reduce.6
  402.3 162.9 all-reduce.8
where the time goes:
time: 718 us; the launch traced here: 717 us
  waiting for transfers between devices  552 us (77%)
  blocking collectives  117 us (16%)
  other arithmetic  20.1 us (3%)
  between operations  17 us (2%)
    unnamed x4, waiting for transfers between devices  541 us
    psum x1, blocking collectives, on_device(): norm_sq = lax.psum(jnp.sum(gsum * gsum), ('shard', 'rep'))  75.3 us
    all_gather x1, blocking collectives, on_device(): lax.all_gather(new_master.astype(jnp.bfloat16), 'rep', axis=0, tiled=True)  41.7 us
  transfers between devices with their start and end apart: 4, of which 4 were waited for; matrix products, arithmetic and copies ran while one was open for 0% of the time, Pallas kernels for 0%

commit v1 on v0

--- a/solution.py
+++ b/solution.py
@@ -46,7 +46,16 @@
     second_fix = 1.0 - jnp.power(jnp.float32(0.95), count)
     update = momentum / first_fix / (jnp.sqrt(variance / second_fix) + 1e-08)
     new_master = master * (1.0 - 0.0001 * 0.1) - 0.0001 * update
-    weights = lax.all_gather(new_master.astype(jnp.bfloat16), "rep", axis=0, tiled=True)
+    panel = new_master.astype(jnp.bfloat16)
+    weights = jnp.concatenate(
+        jax.lax.all_to_all(
+            jnp.stack([panel] * jax.lax.axis_size("rep"), 0),
+            axis_name="rep",
+            split_axis=0,
+            concat_axis=0,
+        ),
+        axis=0,
+    )
 
     def slot_max(values):
         padded = jnp.pad(jnp.abs(values), (half_len, half_len))

time: 718 us -> 696 us (0.969)
  blocking collectives: 117 us -> 90 us
    all_gather x1 -> x0, blocking collectives: 41.7 us -> none  [on_device(): lax.all_gather(new_master.astype(jnp.bfloat16), 'rep', axis=0, tiled=True)]
    all_to_all x0 -> x1, blocking collectives: none -> 14.6 us  [on_device(): jax.lax.all_to_all(jnp.stack([panel] * jax.lax.axis_size('rep'), 0), axis...]
where the time goes in v1:
time: 696 us; the launch traced here: 695 us
  waiting for transfers between devices  552 us (79%)
  blocking collectives  90 us (13%)
  other arithmetic  23.8 us (3%)
  between operations  17 us (2%)
  local copies, waits for them, and re-layouts  8.5 us (1%)
    unnamed x4, waiting for transfers between devices  541 us
    psum x1, blocking collectives, on_device(): norm_sq = lax.psum(jnp.sum(gsum * gsum), ('shard', 'rep'))  75.3 us
    all_to_all x1, blocking collectives, on_device(): jax.lax.all_to_all(jnp.stack([panel] * jax.lax.axis_size('rep'), 0), axis...  14.6 us
  transfers between devices with their start and end apart: 4, of which 4 were waited for; matrix products, arithmetic and copies ran while one was open for 0% of the time, Pallas kernels for 0%

profile of v1, /device:TPU:2, one launch (start us, length us, event | category | flops | bytes accessed | tf_op | source)
XLA Modules:
  0.0 695.1 jit_solution(493162126669365185)
XLA Ops:
  7.2 10.8 %convert_element_type.28 = f32[1,1,2097152]{2,1,0:T(1,128)} convert(bf16[1,1,2097152]{2,1,0:T(2,128)(2,1)} %param.15) | non-fusion elementwise | flops 2097152 | bytes 12582912 | tf_op jit(solution)/shard_map/convert_element_type | solution.py:29
  20.0 379.7 %all-reduce.7.cloned.1.call-done = f32[2097152]{0:T(1024)} async-done(((f32[2097152]{0:T(1024)}), f32[2097152]{0:T(1024)}) %all-reduce.7.cloned.1.call-update) | async-done | bytes 8388624
  399.7 1.9 dynamic-slice.25
  401.6 0.6 dynamic-slice.26
  403.8 161.5 %all-reduce.9.cloned.1.call-done = f32[131072]{0:T(1024)} async-done(((f32[131072]{0:T(1024)}), f32[131072]{0:T(1024)}) %all-reduce.9.cloned.1.call-update) | async-done | bytes 524304
  565.3 1.4 multiply_reduce_fusion
  566.6 75.3 %psum.7 = f32[]{:T(128)} all-reduce(f32[]{:T(128)} %multiply_reduce_fusion), channel_id=1, replica_groups=mesh['shard'=16,'rep'=16] {'shard','rep'}, use_global_device_ids=true, to_apply=%region_3.0 | all-reduce | flops 1 | bytes 8 | tf_op jit(solution)/shard_map/psum | solution.py:32
  642.7 0.8 fusion.6
  643.7 0.6 slice.84
  644.4 0.6 slice.83
  645.0 1.4 maximum_bitcast_fusion
  646.4 1.9 collective-permute-start
  648.3 7.2 %collective-permute-done = f32[1,2]{1,0:T(1,128)S(1)} collective-permute-done((f32[1,2]{1,0:T(1,128)S(1)}, f32[1,2]{1,0:T(1,128)S(1)}, u32[]{:S(2)}, u32[]{:S(2)}) %collective-permute-start) | collective-permute-done | bytes 40 | tf_op jit(solution)/shard_map/ppermute | solution.py:14
  656.0 1.8 constant_dynamic-update-slice_fusion.2
  657.8 1.4 maximum_bitcast_fusion.1
  659.2 1.9 collective-permute-start.1
  661.1 3.5 collective-permute-done.1
  665.2 0.8 constant_dynamic-update-slice_fusion
  666.1 0.8 constant_dynamic-update-slice_fusion.1
  667.0 0.7 fusion.10
  668.6 2.2 reduce.9
  671.0 14.6 %all_to_all.6 = bf16[16,2,4096]{2,1,0:T(2,128)(2,1)S(1)} all-to-all(bf16[16,2,4096]{2,1,0:T(2,128)(2,1)S(1)} %reshape.155), channel_id=1, replica_groups=mesh['shard'=16,'rep'=16] {'rep'}, dimensions={0} | all-to-all | bytes 524288 | tf_op jit(solution)/shard_map/all_to_all | solution.py:51
  685.9 1.5 reduce.8
  687.5 0.8 copy.14
  (43 shorter events, 4.5 us)
Async XLA Ops:
  7.2 392.5 %all-reduce.7.cloned.1.call-start = ((), (), s32[]{:S(2)}) async-start(), calls=%async_computation.1 | async-start | bytes 16777216
  18.0 0.7 copy-start.8
  18.0 383.6 %copy-start.7 = (u32[256]{0:T(256)S(1)}, u32[256]{0:T(256)}, u32[]{:S(2)}) copy-start(u32[256]{0:T(256)} %constant.134) | copy-start | bytes 3076
  18.1 384.2 %copy-start.5 = (f32[5]{0:T(128)S(1)}, f32[5]{0:T(128)}, u32[]{:S(2)}) copy-start(f32[5]{0:T(128)} %param.19) | copy-start | bytes 64
  18.1 384.3 %copy-start.6 = (f32[5]{0:T(128)S(1)}, f32[5]{0:T(128)}, u32[]{:S(2)}) copy-start(f32[5]{0:T(128)} %param.18) | copy-start | bytes 64
  18.1 624.6 %copy-start = (s32[8192]{0:T(1024)S(1)}, s32[8192]{0:T(1024)}, u32[]{:S(2)}) copy-start(s32[8192]{0:T(1024)} %param.17) | copy-start | bytes 98308
  18.1 624.6 %copy-start.1 = (s32[8192]{0:T(1024)S(1)}, s32[8192]{0:T(1024)}, u32[]{:S(2)}) copy-start(s32[8192]{0:T(1024)} %param.16) | copy-start | bytes 98308
  18.1 648.9 %copy-start.2 = (f32[8192]{0:T(1024)S(1)}, f32[8192]{0:T(1024)}, u32[]{:S(2)}) copy-start(f32[8192]{0:T(1024)} %param.20) | copy-start | bytes 98308
  18.1 547.1 %all-reduce.9.cloned.1.call-start = ((), (), s32[]{:S(2)}) async-start(), calls=%async_computation.2 | async-start | bytes 1048576
  646.4 9.1 %collective-permute-start = (f32[1,2]{1,0:T(1,128)S(1)}, f32[1,2]{1,0:T(1,128)S(1)}, u32[]{:S(2)}, u32[]{:S(2)}) collective-permute-start(f32[1,2]{1,0:T(1,128)S(1)} %maximum_bitcast_fusion), channel_id=1, source_target_pairs={{0,1},{1,2},{2,3},{3,4},{4,5},{5,6},{6,7},{7,8},{8,9},{9,10},{10,1... | collective-permute-start | bytes 32 | tf_op jit(solution)/shard_map/ppermute | solution.py:14
  659.2 5.5 collective-permute-start.1
  666.0 22.2 %copy-start.3 = (f32[5]{0:T(128)}, f32[5]{0:T(128)S(1)}, u32[]{:S(2)}) copy-start(f32[5]{0:T(128)S(1)} %constant_dynamic-update-slice_fusion) | copy-start | bytes 64
  666.9 21.3 %copy-start.4 = (f32[5]{0:T(128)}, f32[5]{0:T(128)S(1)}, u32[]{:S(2)}) copy-start(f32[5]{0:T(128)S(1)} %constant_dynamic-update-slice_fusion.1) | copy-start | bytes 64
Sparse Core Ops, SparseCore 0:
  18.3 381.3 all-reduce.6
  402.3 162.9 all-reduce.8
